TPU v7x, 128 devices: a whole 4x4x4 slice. The times are simulated.
128 devices in a mesh: rows: 16 (over z_lo, x, core), cols: 8 (over z_hi, y).
Axes of the slice: x: 4, y: 4, z: 4 (z_hi: 2, z_lo: 2; z = z_hi * 2 + z_lo), core: 2. Of those that a mesh axis runs over, the one named last changes fastest.
Arguments:
- spectrum: bfloat16 [2, 4096, 4096], P(None, 'rows', 'cols'), may hold values from -6 to 6
- diffraction: bfloat16 [2, 32, 3, 128, 128], P(None, 'rows'), may hold values from -0.21875 to 0.21875
- order_mask: int32 [32, 3], P('rows'), may hold values from 0 to 1, as said below
- phases: float32 [2, 4096, 4096], P(None, 'rows', 'cols'), may hold values from -3.140625 to 3.140625
- transmission: float32 [4096, 4096], P('rows', 'cols'), may hold values from 0.2 to 1
- shifts: int32 [2], replicated, may hold values from 128 to 256, as said below
Outputs:
- outgoing: float32 [2, 4096, 4096], P(None, 'rows', 'cols')
Inputs may be any that keep to these rules, and one draw needn't show every extreme that they name: Each bounce's shift lies between 128 and 256; one bounce shifts by exactly 256. `order_mask`: every block carries the orders -1 and +1; the order 0 is off in some blocks.
All inputs are finite; a program needn't handle non-finite values.
Results may differ from a plain program's by a relative error of at most 0.018.
Values may be sent and summed in bfloat16 or wider, within the bound.
A program may use at most 128 MiB of HBM per device.

v0:
```python
import math
import jax
import jax.numpy as jnp
from jax import lax
from jax.sharding import PartitionSpec as P

BLOCK = 128
BASE = 256
BOUNCES = 2


def shifted(value, axis, steps):
    count = lax.axis_size(axis)
    first, last = (max(0, -steps), min(count, count - steps))
    return lax.ppermute(value, axis, [(source, source + steps) for source in range(first, last)])


def twiddles(extent, sign_value, left_index, right_index):
    wrapped = left_index[:, None] * right_index[None, :] % extent
    angles = wrapped.astype(jnp.float32) * (2.0 * math.pi / extent)
    return (jnp.cos(angles), sign_value * jnp.sin(angles))


def base_tables(target, extent, sign_value):
    turn_real, turn_imag = twiddles(extent, sign_value, jnp.arange(BASE, dtype=jnp.int32), target)
    factor = 1.0 / math.sqrt(extent)
    return ((turn_real * factor).astype(jnp.bfloat16), (turn_imag * factor).astype(jnp.bfloat16))


def blocked_dft(values, axis_at, sign_value, target, extent):
    block_count = values.shape[axis_at] // BASE
    base_real, base_imag = base_tables(target, extent, sign_value)
    if axis_at == 1:
        shaped = values.reshape(2, block_count, BASE, values.shape[2])
        form_text = "sio,ik->sko"
    else:
        shaped = values.reshape(2, values.shape[1], block_count, BASE)
        form_text = "osi,ik->sok"

    def contract(left_side, right_side):
        return jnp.einsum(form_text, left_side, right_side, preferred_element_type=jnp.float32)

    inner_real = contract(shaped[0], base_real) - contract(shaped[1], base_imag)
    inner_imag = contract(shaped[0], base_imag) + contract(shaped[1], base_real)
    numbers = jnp.arange(block_count, dtype=jnp.int32) * BASE
    turn_real, turn_imag = twiddles(extent, sign_value, numbers, target)
    if axis_at == 1:
        turn_real = turn_real[:, :, None]
        turn_imag = turn_imag[:, :, None]
    else:
        turn_real = turn_real[:, None, :]
        turn_imag = turn_imag[:, None, :]
    out_real = jnp.sum(turn_real * inner_real - turn_imag * inner_imag, axis=0)
    out_imag = jnp.sum(turn_real * inner_imag + turn_imag * inner_real, axis=0)
    return jnp.stack([out_real, out_imag])


def apply_blocks(left_side, right_side):
    return jnp.einsum("bjk,bkq->bjq", left_side, right_side, preferred_element_type=jnp.float32)


def diffract(current, offset_step, matrices, weights):
    below_rows = shifted(current, "rows", 1)
    above_rows = shifted(current, "rows", -1)
    widened = jnp.concatenate([below_rows, current, above_rows], axis=1)
    height = current.shape[1]
    columns = current.shape[2]
    block_count = height // BLOCK
    result_real = jnp.zeros((block_count, BLOCK, columns), jnp.float32)
    result_imag = jnp.zeros((block_count, BLOCK, columns), jnp.float32)
    for order_at in range(3):
        source = lax.dynamic_slice_in_dim(widened, height + (order_at - 1) * offset_step, height, 1)
        source = source.reshape(2, block_count, BLOCK, columns)
        kernel = matrices[:, :, order_at]
        weight_now = weights[:, order_at][:, None, None]
        result_real = result_real + weight_now * (
            apply_blocks(kernel[0], source[0]) - apply_blocks(kernel[1], source[1])
        )
        result_imag = result_imag + weight_now * (
            apply_blocks(kernel[0], source[1]) + apply_blocks(kernel[1], source[0])
        )
    return (result_real.reshape(height, columns), result_imag.reshape(height, columns))


def on_device(spectrum, diffraction, order_mask, phases, transmission, shifts):
    local_rows = spectrum.shape[1]
    local_cols = spectrum.shape[2]
    row_count = lax.axis_size("rows")
    col_count = lax.axis_size("cols")
    full_rows = local_rows * row_count
    full_cols = local_cols * col_count
    own_rows = lax.axis_index("rows") * local_rows + jnp.arange(local_rows, dtype=jnp.int32)
    own_cols = lax.axis_index("cols") * local_cols + jnp.arange(local_cols, dtype=jnp.int32)
    weights = order_mask.astype(jnp.float32)

    def rows_gather(values, sign_value):
        summed = blocked_dft(
            lax.all_gather(values, "rows", axis=1, tiled=True), 1, sign_value, own_rows, full_rows
        )
        return summed.astype(jnp.bfloat16)

    def columns_gather(values, sign_value):
        return blocked_dft(
            lax.all_gather(values, "cols", axis=2, tiled=True), 2, sign_value, own_cols, full_cols
        )

    current = spectrum
    outgoing = None
    for bounce in range(BOUNCES):
        closing = bounce == BOUNCES - 1
        diff_real, diff_imag = diffract(current, shifts[bounce], diffraction, weights)
        cosine = jnp.cos(phases[bounce])
        sine_part = jnp.sin(phases[bounce])
        wave_k = jnp.stack(
            [diff_real * cosine - diff_imag * sine_part, diff_real * sine_part + diff_imag * cosine]
        ).astype(jnp.bfloat16)
        rows_space = rows_gather(wave_k, 1.0)
        space = columns_gather(rows_space, 1.0) * transmission[None]
        if closing:
            outgoing = space
        else:
            columns_k = columns_gather(space.astype(jnp.bfloat16), -1.0).astype(jnp.bfloat16)
            current = rows_gather(columns_k, -1.0)
    return outgoing


def solution(mesh):
    placed = (
        P(None, "rows", "cols"),
        P(None, "rows", None, None, None),
        P("rows", None),
        P(None, "rows", "cols"),
        P("rows", "cols"),
        P(),
    )
    return jax.shard_map(
        on_device, mesh=mesh, in_specs=placed, out_specs=P(None, "rows", "cols"), check_vma=False
    )
```

profile of v0, /device:TPU:0, one launch (start us, length us, event | category | flops | bytes accessed | tf_op | source)
XLA Modules:
  0.0 625.4 jit_solution(12232110755991861289)
XLA Ops:
  6.5 1.4 collective-permute-start
  14.5 1.4 fusion.322
  20.3 2.0 fusion.57
  24.1 58.0 %all-gather.7.cloned.1.call-done = bf16[2,4096,512]{2,1,0:T(8,128)(2,1)} async-done(((bf16[2,256,512]{2,1,0:T(8,128)(2,1)}), bf16[2,4096,512]{2,1,0:T(8,128)(2,1)}) %all-gather.7.cloned.1.call-update) | async-done | bytes 8388624 | tf_op jit(solution)/shard_map/all_gather | solution.py:98
  82.1 3.8 fusion.317
  85.8 2.2 fusion.109
  88.1 2.3 fusion.119
  90.3 2.2 fusion.111
  92.6 6.7 %fusion.21 = (bf16[256,512]{1,0:T(8,128)(2,1)S(1)}, bf16[256,512]{1,0:T(8,128)(2,1)S(1)}) fusion(f32[16,256]{1,0:T(8,128)S(1)} %get-tuple-element.50, f32[16,256]{1,0:T(8,128)S(1)} %get-tuple-element.51, f32[256,16,512]{2,0,1:T(8,128)S(1)} %fusion.109, f32[256,16,512]{2,0,1:T(8,128)S(1)} %fusion.111, f32[256,16,512]{2,0,1:T(8,128)S(1)} %fusion.119, ...), kind=kOutput, calls=%fused_computation.43 | convolution fusion | flops 1095499776 | bytes 29918208 | tf_op jit(solution)/shard_map/sio,ik->sko/dot_general | solution.py:41
  101.6 76.9 %all-gather.9.cloned.1.call-done = bf16[2,256,4096]{2,1,0:T(8,128)(2,1)} async-done(((bf16[2,256,512]{2,1,0:T(8,128)(2,1)}), bf16[2,256,4096]{2,1,0:T(8,128)(2,1)}) %all-gather.9.cloned.1.call-update) | async-done | bytes 4194320 | tf_op jit(solution)/shard_map/all_gather | solution.py:104
  178.4 4.7 fusion.320
  183.1 3.3 copy.41
  186.4 5.4 fusion.80
  191.8 5.4 fusion.90
  197.1 3.3 copy.39
  200.4 3.1 fusion.82
  203.8 10.2 %fusion.17 = (f32[256,512]{0,1:T(8,128)S(1)}, f32[256,512]{0,1:T(8,128)S(1)}) fusion(f32[16,512]{1,0:T(8,128)S(1)} %get-tuple-element.47, f32[16,512]{1,0:T(8,128)S(1)} %get-tuple-element.48, f32[512,256,16]{1,0,2:T(8,128)} %fusion.80, f32[512,256,16]{1,0,2:T(8,128)S(1)} %fusion.82, f32[512,256,16]{1,0,2:T(8,128)S(1)} %copy-done.1, ...), kind=kOutput, calls=%fused_computation.35 | convolution fusion | flops 1096548352 | bytes 28379136 | tf_op jit(solution)/shard_map/osi,ik->sok/dot_general | solution.py:41
  215.5 69.9 %all-gather.11.cloned.1.call-done = bf16[2,256,4096]{1,2,0:T(8,128)(2,1)} async-done(((bf16[2,256,512]{1,2,0:T(8,128)(2,1)}), bf16[2,256,4096]{1,2,0:T(8,128)(2,1)}) %all-gather.11.cloned.1.call-update) | async-done | bytes 4194320 | tf_op jit(solution)/shard_map/all_gather | solution.py:104
  285.4 2.5 fusion.319
  287.9 3.1 fusion.76
  291.0 3.1 fusion.94
  294.2 3.1 fusion.78
  297.3 8.7 %fusion.13 = (bf16[256,512]{0,1:T(8,128)(2,1)S(1)}, bf16[256,512]{0,1:T(8,128)(2,1)S(1)}) fusion(f32[16,512]{1,0:T(8,128)S(1)} %get-tuple-element.46, f32[16,512]{1,0:T(8,128)S(1)} %get-tuple-element.48, f32[512,256,16]{1,0,2:T(8,128)S(1)} %fusion.76, f32[512,256,16]{1,0,2:T(8,128)S(1)} %fusion.78, f32[512,256,16]{1,0,2:T(8,128)S(1)} %fusion.94, ...), kind=kOutput, calls=%fused_computation.27 | convolution fusion | flops 1096548352 | bytes 27854848 | tf_op jit(solution)/shard_map/osi,ik->sok/dot_general | solution.py:41
  307.1 58.6 %all-gather.13.cloned.1.call-done = bf16[2,4096,512]{1,2,0:T(8,128)(2,1)} async-done(((bf16[2,256,512]{1,2,0:T(8,128)(2,1)}), bf16[2,4096,512]{1,2,0:T(8,128)(2,1)}) %all-gather.13.cloned.1.call-update) | async-done | bytes 8388624 | tf_op jit(solution)/shard_map/all_gather | solution.py:98
  365.8 6.0 fusion.316
  371.8 6.5 %copy.51 = bf16[1,4096,512]{2,1,0:T(8,128)(2,1)} copy(bf16[1,4096,512]{1,2,0:T(8,128)(2,1)} %get-tuple-element.22) | data formatting | bytes 8388608 | tf_op jit(solution)/shard_map/slice | solution.py:43
  378.2 7.8 %fusion.105 = f32[256,16,512]{2,0,1:T(8,128)} fusion(bf16[16,256,512]{2,1,0:T(8,128)(2,1)} %bitcast.390, s32[256]{0:T(256)S(1)} %copy-done.12), kind=kOutput, calls=%fused_computation.166 | convolution fusion | flops 1074790400 | bytes 12583936 | tf_op jit(solution)/shard_map/sio,ik->sko/dot_general | solution.py:41
  386.0 5.5 fusion.123
  391.5 6.5 %copy.50 = bf16[1,4096,512]{2,1,0:T(8,128)(2,1)} copy(bf16[1,4096,512]{1,2,0:T(8,128)(2,1)} %get-tuple-element.23) | data formatting | bytes 8388608 | tf_op jit(solution)/shard_map/slice | solution.py:43
  398.1 4.6 fusion.107
  402.7 1.3 copy-done.4
  404.0 8.0 %fusion.9 = (bf16[256,512]{1,0:T(8,128)(2,1)S(1)}, bf16[256,512]{1,0:T(8,128)(2,1)S(1)}) fusion(f32[16,256]{1,0:T(8,128)S(1)} %copy-done.15, f32[16,256]{1,0:T(8,128)S(1)} %get-tuple-element.51, f32[256,16,512]{2,0,1:T(8,128)} %fusion.105, f32[256,16,512]{2,0,1:T(8,128)S(1)} %fusion.107, f32[256,16,512]{2,0,1:T(8,128)S(1)} %copy-done.4, ...), kind=kOutput, calls=%fused_computation.19 | convolution fusion | flops 1095499776 | bytes 29918208 | tf_op jit(solution)/shard_map/sio,ik->sko/dot_general | solution.py:41
  413.3 3.8 collective-permute-start.2
  424.2 2.1 fusion.53
  427.5 57.0 %all-gather.15.cloned.1.call-done = bf16[2,4096,512]{2,1,0:T(8,128)(2,1)} async-done(((bf16[2,256,512]{2,1,0:T(8,128)(2,1)}), bf16[2,4096,512]{2,1,0:T(8,128)(2,1)}) %all-gather.15.cloned.1.call-update) | async-done | bytes 8388624 | tf_op jit(solution)/shard_map/all_gather | solution.py:98
  484.4 3.8 fusion.315
  488.2 2.2 fusion.101
  490.5 2.3 fusion.115
  492.7 2.2 fusion.103
  495.0 6.7 %fusion.5 = (bf16[256,512]{1,0:T(8,128)(2,1)S(1)}, bf16[256,512]{1,0:T(8,128)(2,1)S(1)}) fusion(f32[16,256]{1,0:T(8,128)S(1)} %copy-done.14, f32[16,256]{1,0:T(8,128)S(1)} %get-tuple-element.51, f32[256,16,512]{2,0,1:T(8,128)S(1)} %fusion.101, f32[256,16,512]{2,0,1:T(8,128)S(1)} %fusion.103, f32[256,16,512]{2,0,1:T(8,128)S(1)} %fusion.115, ...), kind=kOutput, calls=%fused_computation.11 | convolution fusion | flops 1095499776 | bytes 29918208 | tf_op jit(solution)/shard_map/sio,ik->sko/dot_general | solution.py:41
  502.5 78.2 %all-gather.17.cloned.1.call-done = bf16[2,256,4096]{2,1,0:T(8,128)(2,1)} async-done(((bf16[2,256,512]{2,1,0:T(8,128)(2,1)}), bf16[2,256,4096]{2,1,0:T(8,128)(2,1)}) %all-gather.17.cloned.1.call-update) | async-done | bytes 4194320 | tf_op jit(solution)/shard_map/all_gather | solution.py:104
  580.8 4.7 fusion.318
  585.5 3.3 copy.54
  588.7 5.4 fusion.72
  594.1 5.4 fusion.86
  599.5 3.5 copy.52
  603.0 3.1 fusion.74
  606.4 10.2 %fusion.1 = (f32[256,512]{0,1:T(8,128)S(1)}, f32[256,512]{0,1:T(8,128)S(1)}) fusion(f32[16,512]{1,0:T(8,128)S(1)} %get-tuple-element.47, f32[16,512]{1,0:T(8,128)S(1)} %get-tuple-element.48, f32[512,256,16]{1,0,2:T(8,128)} %fusion.72, f32[512,256,16]{1,0,2:T(8,128)S(1)} %fusion.74, f32[512,256,16]{1,0,2:T(8,128)S(1)} %copy-done, ...), kind=kOutput, calls=%fused_computation.3 | convolution fusion | flops 1096548352 | bytes 28379136 | tf_op jit(solution)/shard_map/osi,ik->sok/dot_general | solution.py:41
  (111 shorter events, 25.3 us)
Async XLA Ops:
  6.5 11.6 %copy-start.6 = (bf16[2,256,512]{2,1,0:T(8,128)(2,1)S(1)}, bf16[2,256,512]{2,1,0:T(8,128)(2,1)}, u32[]{:S(2)}) copy-start(bf16[2,256,512]{2,1,0:T(8,128)(2,1)} %param.6) | copy-start | bytes 1572868
  6.5 11.3 %copy-start.5 = (bf16[2,2,3,128,128]{4,3,2,1,0:T(8,128)(2,1)S(1)}, bf16[2,2,3,128,128]{4,3,2,1,0:T(8,128)(2,1)}, u32[]{:S(2)}) copy-start(bf16[2,2,3,128,128]{4,3,2,1,0:T(8,128)(2,1)} %param.7) | copy-start | bytes 1179652
  6.5 75.5 %all-gather.7.cloned.1.call-start = ((), (), s32[]{:S(2)}) async-start(), calls=%async_computation | async-start | bytes 8912896 | tf_op jit(solution)/shard_map/all_gather | solution.py:98
  6.5 11.5 %collective-permute-start = (bf16[2,256,512]{2,1,0:T(8,128)(2,1)}, bf16[2,256,512]{2,1,0:T(8,128)(2,1)S(1)}, u32[]{:S(2)}, u32[]{:S(2)}) collective-permute-start(bf16[2,256,512]{2,1,0:T(8,128)(2,1)} %param.6), channel_id=1, source_target_pairs={{0,8},{8,16},{16,24},{24,32},{32,40},{40,48},{48,56},{56,64},{64,7... | collective-permute-start | bytes 1572872 | tf_op jit(solution)/shard_map/ppermute | solution.py:15
  8.0 10.2 %collective-permute-start.1 = (bf16[2,256,512]{2,1,0:T(8,128)(2,1)}, bf16[2,256,512]{2,1,0:T(8,128)(2,1)S(1)}, u32[]{:S(2)}, u32[]{:S(2)}) collective-permute-start(bf16[2,256,512]{2,1,0:T(8,128)(2,1)} %param.6), channel_id=1, source_target_pairs={{8,0},{16,8},{24,16},{32,24},{40,32},{48,40},{56,48},{64,56},{72,6... | collective-permute-start | bytes 1572872 | tf_op jit(solution)/shard_map/ppermute | solution.py:15
  11.3 7.2 %copy-start.16 = (f32[2]{0:T(128)}, f32[2]{0:T(128)S(1)}, u32[]{:S(2)}) copy-start(f32[2]{0:T(128)S(1)} %get-tuple-element.18) | copy-start | bytes 28
  11.3 8.3 %copy-start.18 = (f32[2]{0:T(128)}, f32[2]{0:T(128)S(1)}, u32[]{:S(2)}) copy-start(f32[2]{0:T(128)S(1)} %get-tuple-element.19) | copy-start | bytes 28
  11.3 8.8 %copy-start.20 = (f32[2]{0:T(128)}, f32[2]{0:T(128)S(1)}, u32[]{:S(2)}) copy-start(f32[2]{0:T(128)S(1)} %get-tuple-element.17) | copy-start | bytes 28
  19.1 1.2 copy-start.7
  23.2 155.2 %all-gather.9.cloned.1.call-start = ((), (), s32[]{:S(2)}) async-start(), calls=%async_computation.1 | async-start | bytes 4718592 | tf_op jit(solution)/shard_map/all_gather | solution.py:104
  23.3 62.6 %copy-start.22 = (s32[16]{0:T(128)}, s32[16]{0:T(128)S(1)}, u32[]{:S(2)}) copy-start(s32[16]{0:T(128)S(1)} %iota_multiply_fusion) | copy-start | bytes 196
  23.3 69.3 %copy-start.11 = (s32[256]{0:T(256)}, s32[256]{0:T(256)S(1)}, u32[]{:S(2)}) copy-start(s32[256]{0:T(256)S(1)} %iota_add_fusion.1) | copy-start | bytes 3076
  24.1 68.5 %copy-start.13 = (f32[16,256]{1,0:T(8,128)}, f32[16,256]{1,0:T(8,128)S(1)}, u32[]{:S(2)}) copy-start(f32[16,256]{1,0:T(8,128)S(1)} %get-tuple-element.50) | copy-start | bytes 49156
  92.6 7.9 %copy-start.9 = (f32[256,512]{1,0:T(8,128)S(1)}, f32[256,512]{1,0:T(8,128)}, u32[]{:S(2)}) copy-start(f32[256,512]{1,0:T(8,128)} %param.10) | copy-start | bytes 1572868
  100.2 185.2 %all-gather.11.cloned.1.call-start = ((), (), s32[]{:S(2)}) async-start(), calls=%async_computation.2 | async-start | bytes 4718592 | tf_op jit(solution)/shard_map/all_gather | solution.py:104
  200.4 3.4 copy-start.1
  215.0 150.8 %all-gather.13.cloned.1.call-start = ((), (), s32[]{:S(2)}) async-start(), calls=%async_computation.3 | async-start | bytes 8912896 | tf_op jit(solution)/shard_map/all_gather | solution.py:98
  306.9 177.5 %all-gather.15.cloned.1.call-start = ((), (), s32[]{:S(2)}) async-start(), calls=%async_computation.4 | async-start | bytes 8912896 | tf_op jit(solution)/shard_map/all_gather | solution.py:98
  371.8 6.5 %copy-start.12 = (s32[256]{0:T(256)S(1)}, s32[256]{0:T(256)}, u32[]{:S(2)}) copy-start(s32[256]{0:T(256)} %copy-done.11) | copy-start | bytes 3076
  378.2 7.8 %copy-start.2 = (bf16[1,4096,512]{2,1,0:T(8,128)(2,1)S(1)}, bf16[1,4096,512]{2,1,0:T(8,128)(2,1)}, u32[]{:S(2)}) copy-start(bf16[1,4096,512]{2,1,0:T(8,128)(2,1)} %copy.51) | copy-start | bytes 12582916
  391.5 11.1 %copy-start.15 = (f32[16,256]{1,0:T(8,128)S(1)}, f32[16,256]{1,0:T(8,128)}, u32[]{:S(2)}) copy-start(f32[16,256]{1,0:T(8,128)} %get-tuple-element.49) | copy-start | bytes 49156
  398.0 4.6 copy-start.3
  398.0 5.9 copy-start.4
  412.0 7.5 %collective-permute-start.3 = (bf16[2,256,512]{2,1,0:T(8,128)(2,1)S(1)}, bf16[2,256,512]{2,1,0:T(8,128)(2,1)S(1)}, u32[]{:S(2)}, u32[]{:S(2)}) collective-permute-start(bf16[2,256,512]{2,1,0:T(8,128)(2,1)S(1)} %pad_maximum_fusion.4), channel_id=1, source_target_pairs={{8,0},{16,8},{24,16},{32,24},{40,32},{48,40},{56,48},{64,56},{72,6... | collective-permute-start | bytes 1572872 | tf_op jit(solution)/shard_map/ppermute | solution.py:15
  413.3 7.0 %collective-permute-start.2 = (bf16[2,256,512]{2,1,0:T(8,128)(2,1)S(1)}, bf16[2,256,512]{2,1,0:T(8,128)(2,1)}, u32[]{:S(2)}, u32[]{:S(2)}) collective-permute-start(bf16[2,256,512]{2,1,0:T(8,128)(2,1)S(1)} %pad_maximum_fusion.4), channel_id=1, source_target_pairs={{0,8},{8,16},{16,24},{24,32},{32,40},{40,48},{48,56},{56,64},{64,7... | collective-permute-start | bytes 1572872 | tf_op jit(solution)/shard_map/ppermute | solution.py:15
  419.1 3.3 copy-start.19
  419.5 0.8 copy-start.10
  421.6 1.6 copy-start.17
  421.9 1.6 copy-start.21
  423.0 1.2 copy-start.8
  427.2 153.6 %all-gather.17.cloned.1.call-start = ((), (), s32[]{:S(2)}) async-start(), calls=%async_computation.5 | async-start | bytes 4718592 | tf_op jit(solution)/shard_map/all_gather | solution.py:104
  492.7 2.3 copy-start.14
  603.0 3.4 copy-start
Sparse Core Ops, SparseCore 0:
  23.3 58.6 all-gather.6
  100.3 78.0 all-gather.8
  215.1 70.2 all-gather.10
  307.0 58.6 all-gather.12
  427.3 57.0 all-gather.14
  502.7 78.0 all-gather.16
where the time goes:
time: 635 us; the launch traced here: 625 us
  waiting for transfers between devices  399 us (63%)
  matrix products  127 us (20%)
  local copies, waits for them, and re-layouts  59.3 us (9%)
  between operations  18.5 us (3%)
  other arithmetic  13 us (2%)
  starting transfers between devices  9.08 us (1%)
    all_gather x3, waiting for transfers between devices, columns_gather(): lax.all_gather(values, 'cols', axis=2, tiled=True)  225 us
    all_gather x3, waiting for transfers between devices, rows_gather(): lax.all_gather(values, 'rows', axis=1, tiled=True)  174 us
    dot_general x24, matrix products, contract(): jnp.einsum(form_text, left_side, right_side, preferred_element_type=jnp.f...  119 us
    slice x12, local copies, waits for them, and re-layouts, blocked_dft(): inner_real = contract(shaped[0], base_real) - contract(shaped[1], base_imag)  51.6 us
  transfers between devices with their start and end apart: 10, of which 6 were waited for; matrix products, arithmetic and copies ran while one was open for 1% of the time, Pallas kernels for 0%

commit v1 on v0

--- a/solution.py
+++ b/solution.py
@@ -101,7 +101,11 @@
 
     def columns_gather(values, sign_value):
         return blocked_dft(
-            lax.all_gather(values, "cols", axis=2, tiled=True), 2, sign_value, own_cols, full_cols
+            jnp.concatenate(lax.all_gather(values, "cols"), axis=2),
+            2,
+            sign_value,
+            own_cols,
+            full_cols,
         )
 
     current = spectrum

time: 635 us -> 604 us (0.951)
  matrix products: 127 us -> 114 us
  waiting for transfers between devices: 399 us -> 389 us
    slice x12 -> x8, local copies, waits for them, and re-layouts: 51.6 us -> 34.2 us  [blocked_dft(): inner_real = contract(shaped[0], base_real) - contract(shaped[1], base_imag)]
    dot_general x24, matrix products: 119 us -> 106 us  [contract(): jnp.einsum(form_text, left_side, right_side, preferred_element_type=jnp.f...]
    all_gather x0 -> x2, local copies, waits for them, and re-layouts: none -> 12.7 us  [columns_gather(): lax.all_gather(values, 'cols')]
    all_gather x3, waiting for transfers between devices: 225 us -> 214 us  [columns_gather(): lax.all_gather(values, 'cols')]
where the time goes in v1:
time: 604 us; the launch traced here: 595 us
  waiting for transfers between devices  389 us (64%)
  matrix products  114 us (19%)
  local copies, waits for them, and re-layouts  53.1 us (9%)
  between operations  18.3 us (3%)
  other arithmetic  11.8 us (2%)
  starting transfers between devices  9.07 us (2%)
    all_gather x3, waiting for transfers between devices, columns_gather(): lax.all_gather(values, 'cols')  214 us
    all_gather x3, waiting for transfers between devices, rows_gather(): lax.all_gather(values, 'rows', axis=1, tiled=True)  175 us
    dot_general x24, matrix products, contract(): jnp.einsum(form_text, left_side, right_side, preferred_element_type=jnp.f...  106 us
    slice x8, local copies, waits for them, and re-layouts, blocked_dft(): inner_real = contract(shaped[0], base_real) - contract(shaped[1], base_imag)  34.2 us
    all_gather x2, local copies, waits for them, and re-layouts, columns_gather(): lax.all_gather(values, 'cols')  12.7 us
  transfers between devices with their start and end apart: 10, of which 6 were waited for; matrix products, arithmetic and copies ran while one was open for 1% of the time, Pallas kernels for 0%

profile of v1, /device:TPU:0, one launch (start us, length us, event | category | flops | bytes accessed | tf_op | source)
XLA Modules:
  0.0 595.0 jit_solution(14376324272591363941)
XLA Ops:
  6.5 1.4 collective-permute-start
  14.4 1.3 fusion.322
  20.3 2.0 fusion.57
  23.4 58.7 %all-gather.7.cloned.1.call-done = bf16[2,4096,512]{2,1,0:T(8,128)(2,1)} async-done(((bf16[2,256,512]{2,1,0:T(8,128)(2,1)}), bf16[2,4096,512]{2,1,0:T(8,128)(2,1)}) %all-gather.7.cloned.1.call-update) | async-done | bytes 8388624 | tf_op jit(solution)/shard_map/all_gather | solution.py:98
  82.0 3.8 fusion.317
  85.8 2.2 fusion.109
  88.0 2.3 fusion.119
  90.3 2.2 fusion.111
  92.6 6.4 %fusion.21 = (bf16[256,512]{1,0:T(8,128)(2,1)S(1)}, bf16[256,512]{1,0:T(8,128)(2,1)S(1)}) fusion(f32[16,256]{1,0:T(8,128)S(1)} %get-tuple-element.50, f32[16,256]{1,0:T(8,128)S(1)} %get-tuple-element.51, f32[256,16,512]{2,0,1:T(8,128)S(1)} %fusion.109, f32[256,16,512]{2,0,1:T(8,128)S(1)} %fusion.111, f32[256,16,512]{2,0,1:T(8,128)S(1)} %fusion.119, ...), kind=kOutput, calls=%fused_computation.43 | convolution fusion | flops 1095499776 | bytes 29918208 | tf_op jit(solution)/shard_map/sio,ik->sko/dot_general | solution.py:41
  100.5 71.9 %all-gather.9.cloned.1.call-done = bf16[8,2,256,512]{3,2,1,0:T(8,128)(2,1)} async-done(((bf16[1,2,256,512]{3,2,1,0:T(8,128)(2,1)}), bf16[8,2,256,512]{3,2,1,0:T(8,128)(2,1)}) %all-gather.9.cloned.1.call-update) | async-done | bytes 4194320 | tf_op jit(solution)/shard_map/all_gather | solution.py:104
  172.4 6.2 %copy.65 = bf16[8,2,256,512]{2,3,0,1:T(8,128)(2,1)} copy(bf16[8,2,256,512]{3,2,1,0:T(8,128)(2,1)} %all-gather.9.cloned.1.call-done) | data formatting | bytes 8388608 | tf_op jit(solution)/shard_map/all_gather | solution.py:104
  178.7 2.6 fusion.320
  181.3 3.1 fusion.80
  184.4 3.2 fusion.90
  187.6 3.1 fusion.82
  190.7 8.7 %fusion.17 = (f32[256,512]{0,1:T(8,128)S(1)}, f32[256,512]{0,1:T(8,128)S(1)}) fusion(f32[16,512]{1,0:T(8,128)S(1)} %get-tuple-element.47, f32[16,512]{1,0:T(8,128)S(1)} %get-tuple-element.48, f32[512,256,16]{1,0,2:T(8,128)S(1)} %fusion.80, f32[512,256,16]{1,0,2:T(8,128)S(1)} %fusion.82, f32[512,256,16]{1,0,2:T(8,128)S(1)} %fusion.90, ...), kind=kOutput, calls=%fused_computation.35 | convolution fusion | flops 1096548352 | bytes 28379136 | tf_op jit(solution)/shard_map/osi,ik->sok/dot_general | solution.py:41
  200.8 69.0 %all-gather.11.cloned.1.call-done = bf16[8,2,256,512]{2,3,0,1:T(8,128)(2,1)} async-done(((bf16[1,2,256,512]{2,3,0,1:T(8,128)(2,1)}), bf16[8,2,256,512]{2,3,0,1:T(8,128)(2,1)}) %all-gather.11.cloned.1.call-update) | async-done | bytes 4194320 | tf_op jit(solution)/shard_map/all_gather | solution.py:104
  269.8 2.6 fusion.319
  272.4 3.1 fusion.76
  275.5 3.1 fusion.94
  278.7 3.1 fusion.78
  281.8 8.7 %fusion.13 = (bf16[256,512]{0,1:T(8,128)(2,1)S(1)}, bf16[256,512]{0,1:T(8,128)(2,1)S(1)}) fusion(f32[16,512]{1,0:T(8,128)S(1)} %get-tuple-element.46, f32[16,512]{1,0:T(8,128)S(1)} %get-tuple-element.48, f32[512,256,16]{1,0,2:T(8,128)S(1)} %fusion.76, f32[512,256,16]{1,0,2:T(8,128)S(1)} %fusion.78, f32[512,256,16]{1,0,2:T(8,128)S(1)} %fusion.94, ...), kind=kOutput, calls=%fused_computation.27 | convolution fusion | flops 1096548352 | bytes 27854848 | tf_op jit(solution)/shard_map/osi,ik->sok/dot_general | solution.py:41
  291.6 58.6 %all-gather.13.cloned.1.call-done = bf16[2,4096,512]{1,2,0:T(8,128)(2,1)} async-done(((bf16[2,256,512]{1,2,0:T(8,128)(2,1)}), bf16[2,4096,512]{1,2,0:T(8,128)(2,1)}) %all-gather.13.cloned.1.call-update) | async-done | bytes 8388624 | tf_op jit(solution)/shard_map/all_gather | solution.py:98
  350.3 6.0 %fusion.316 = (bf16[1,4096,512]{1,2,0:T(8,128)(2,1)}, bf16[1,4096,512]{1,2,0:T(8,128)(2,1)}) fusion(bf16[2,4096,512]{1,2,0:T(8,128)(2,1)} %all-gather.13.cloned.1.call-done), kind=kLoop, calls=%fused_computation.396 | loop fusion | bytes 16777216 | tf_op jit(solution)/shard_map/slice | solution.py:43
  356.2 6.5 %copy.76 = bf16[1,4096,512]{2,1,0:T(8,128)(2,1)} copy(bf16[1,4096,512]{1,2,0:T(8,128)(2,1)} %get-tuple-element.22) | data formatting | bytes 8388608 | tf_op jit(solution)/shard_map/slice | solution.py:43
  362.7 7.8 %fusion.105 = f32[256,16,512]{2,0,1:T(8,128)} fusion(bf16[16,256,512]{2,1,0:T(8,128)(2,1)} %bitcast.393, s32[256]{0:T(256)S(1)} %iota_add_fusion.1), kind=kOutput, calls=%fused_computation.166 | convolution fusion | flops 1074790400 | bytes 12583936 | tf_op jit(solution)/shard_map/sio,ik->sko/dot_general | solution.py:41
  370.5 5.5 fusion.123
  376.0 6.5 %copy.75 = bf16[1,4096,512]{2,1,0:T(8,128)(2,1)} copy(bf16[1,4096,512]{1,2,0:T(8,128)(2,1)} %get-tuple-element.23) | data formatting | bytes 8388608 | tf_op jit(solution)/shard_map/slice | solution.py:43
  382.5 4.6 fusion.107
  387.1 1.3 copy-done.2
  388.4 8.0 %fusion.9 = (bf16[256,512]{1,0:T(8,128)(2,1)S(1)}, bf16[256,512]{1,0:T(8,128)(2,1)S(1)}) fusion(f32[16,256]{1,0:T(8,128)S(1)} %get-tuple-element.49, f32[16,256]{1,0:T(8,128)S(1)} %get-tuple-element.51, f32[256,16,512]{2,0,1:T(8,128)} %fusion.105, f32[256,16,512]{2,0,1:T(8,128)S(1)} %fusion.107, f32[256,16,512]{2,0,1:T(8,128)S(1)} %copy-done.2, ...), kind=kOutput, calls=%fused_computation.19 | convolution fusion | flops 1095499776 | bytes 29918208 | tf_op jit(solution)/shard_map/sio,ik->sko/dot_general | solution.py:41
  397.7 3.8 collective-permute-start.2
  403.9 1.3 pad_maximum_fusion
  407.7 2.1 fusion.53
  410.9 57.8 %all-gather.15.cloned.1.call-done = bf16[2,4096,512]{2,1,0:T(8,128)(2,1)} async-done(((bf16[2,256,512]{2,1,0:T(8,128)(2,1)}), bf16[2,4096,512]{2,1,0:T(8,128)(2,1)}) %all-gather.15.cloned.1.call-update) | async-done | bytes 8388624 | tf_op jit(solution)/shard_map/all_gather | solution.py:98
  468.7 3.8 fusion.315
  472.5 2.2 fusion.101
  474.7 2.2 fusion.115
  477.0 2.2 fusion.103
  479.2 6.4 %fusion.5 = (bf16[256,512]{1,0:T(8,128)(2,1)S(1)}, bf16[256,512]{1,0:T(8,128)(2,1)S(1)}) fusion(f32[16,256]{1,0:T(8,128)S(1)} %get-tuple-element.50, f32[16,256]{1,0:T(8,128)S(1)} %get-tuple-element.51, f32[256,16,512]{2,0,1:T(8,128)S(1)} %fusion.101, f32[256,16,512]{2,0,1:T(8,128)S(1)} %fusion.103, f32[256,16,512]{2,0,1:T(8,128)S(1)} %fusion.115, ...), kind=kOutput, calls=%fused_computation.11 | convolution fusion | flops 1095499776 | bytes 29918208 | tf_op jit(solution)/shard_map/sio,ik->sko/dot_general | solution.py:41
  486.4 72.6 %all-gather.17.cloned.1.call-done = bf16[8,2,256,512]{3,2,1,0:T(8,128)(2,1)} async-done(((bf16[1,2,256,512]{3,2,1,0:T(8,128)(2,1)}), bf16[8,2,256,512]{3,2,1,0:T(8,128)(2,1)}) %all-gather.17.cloned.1.call-update) | async-done | bytes 4194320 | tf_op jit(solution)/shard_map/all_gather | solution.py:104
  559.1 6.5 %copy.77 = bf16[8,2,256,512]{2,3,0,1:T(8,128)(2,1)} copy(bf16[8,2,256,512]{3,2,1,0:T(8,128)(2,1)} %all-gather.17.cloned.1.call-done) | data formatting | bytes 8388608 | tf_op jit(solution)/shard_map/all_gather | solution.py:104
  565.6 2.6 fusion.318
  568.2 3.1 fusion.72
  571.3 3.2 fusion.86
  574.5 3.1 fusion.74
  577.6 8.7 %fusion.1 = (f32[256,512]{0,1:T(8,128)S(1)}, f32[256,512]{0,1:T(8,128)S(1)}) fusion(f32[16,512]{1,0:T(8,128)S(1)} %get-tuple-element.47, f32[16,512]{1,0:T(8,128)S(1)} %get-tuple-element.48, f32[512,256,16]{1,0,2:T(8,128)S(1)} %fusion.72, f32[512,256,16]{1,0,2:T(8,128)S(1)} %fusion.74, f32[512,256,16]{1,0,2:T(8,128)S(1)} %fusion.86, ...), kind=kOutput, calls=%fused_computation.3 | convolution fusion | flops 1096548352 | bytes 28379136 | tf_op jit(solution)/shard_map/osi,ik->sok/dot_general | solution.py:41
  586.4 1.3 copy.83
  (77 shorter events, 20.1 us)
Async XLA Ops:
  6.5 11.5 %copy-start.4 = (bf16[2,256,512]{2,1,0:T(8,128)(2,1)S(1)}, bf16[2,256,512]{2,1,0:T(8,128)(2,1)}, u32[]{:S(2)}) copy-start(bf16[2,256,512]{2,1,0:T(8,128)(2,1)} %param.6) | copy-start | bytes 1572868
  6.5 11.2 %copy-start.3 = (bf16[2,2,3,128,128]{4,3,2,1,0:T(8,128)(2,1)S(1)}, bf16[2,2,3,128,128]{4,3,2,1,0:T(8,128)(2,1)}, u32[]{:S(2)}) copy-start(bf16[2,2,3,128,128]{4,3,2,1,0:T(8,128)(2,1)} %param.7) | copy-start | bytes 1179652
  6.5 75.5 %all-gather.7.cloned.1.call-start = ((), (), s32[]{:S(2)}) async-start(), calls=%async_computation | async-start | bytes 8912896 | tf_op jit(solution)/shard_map/all_gather | solution.py:98
  6.5 11.4 %collective-permute-start = (bf16[2,256,512]{2,1,0:T(8,128)(2,1)}, bf16[2,256,512]{2,1,0:T(8,128)(2,1)S(1)}, u32[]{:S(2)}, u32[]{:S(2)}) collective-permute-start(bf16[2,256,512]{2,1,0:T(8,128)(2,1)} %param.6), channel_id=1, source_target_pairs={{0,8},{8,16},{16,24},{24,32},{32,40},{40,48},{48,56},{56,64},{64,7... | collective-permute-start | bytes 1572872 | tf_op jit(solution)/shard_map/ppermute | solution.py:15
  8.0 10.1 %collective-permute-start.1 = (bf16[2,256,512]{2,1,0:T(8,128)(2,1)}, bf16[2,256,512]{2,1,0:T(8,128)(2,1)S(1)}, u32[]{:S(2)}, u32[]{:S(2)}) collective-permute-start(bf16[2,256,512]{2,1,0:T(8,128)(2,1)} %param.6), channel_id=1, source_target_pairs={{8,0},{16,8},{24,16},{32,24},{40,32},{48,40},{56,48},{64,56},{72,6... | collective-permute-start | bytes 1572872 | tf_op jit(solution)/shard_map/ppermute | solution.py:15
  19.0 1.2 copy-start.5
  23.1 149.3 %all-gather.9.cloned.1.call-start = ((), (), s32[]{:S(2)}) async-start(), calls=%async_computation.1 | async-start | bytes 4718592 | tf_op jit(solution)/shard_map/all_gather | solution.py:104
  92.5 7.5 %copy-start.6 = (f32[256,512]{1,0:T(8,128)S(1)}, f32[256,512]{1,0:T(8,128)}, u32[]{:S(2)}) copy-start(f32[256,512]{1,0:T(8,128)} %param.10) | copy-start | bytes 1572868
  99.8 170.0 %all-gather.11.cloned.1.call-start = ((), (), s32[]{:S(2)}) async-start(), calls=%async_computation.2 | async-start | bytes 4718592 | tf_op jit(solution)/shard_map/all_gather | solution.py:104
  200.3 149.9 %all-gather.13.cloned.1.call-start = ((), (), s32[]{:S(2)}) async-start(), calls=%async_computation.3 | async-start | bytes 8912896 | tf_op jit(solution)/shard_map/all_gather | solution.py:98
  291.4 177.3 %all-gather.15.cloned.1.call-start = ((), (), s32[]{:S(2)}) async-start(), calls=%async_computation.4 | async-start | bytes 8912896 | tf_op jit(solution)/shard_map/all_gather | solution.py:98
  362.7 7.8 %copy-start = (bf16[1,4096,512]{2,1,0:T(8,128)(2,1)S(1)}, bf16[1,4096,512]{2,1,0:T(8,128)(2,1)}, u32[]{:S(2)}) copy-start(bf16[1,4096,512]{2,1,0:T(8,128)(2,1)} %copy.76) | copy-start | bytes 12582916
  382.5 4.6 copy-start.1
  382.5 5.9 copy-start.2
  396.4 7.5 %collective-permute-start.3 = (bf16[2,256,512]{2,1,0:T(8,128)(2,1)S(1)}, bf16[2,256,512]{2,1,0:T(8,128)(2,1)}, u32[]{:S(2)}, u32[]{:S(2)}) collective-permute-start(bf16[2,256,512]{2,1,0:T(8,128)(2,1)S(1)} %pad_maximum_fusion.4), channel_id=1, source_target_pairs={{8,0},{16,8},{24,16},{32,24},{40,32},{48,40},{56,48},{64,56},{72,6... | collective-permute-start | bytes 1572872 | tf_op jit(solution)/shard_map/ppermute | solution.py:15
  397.7 6.2 %collective-permute-start.2 = (bf16[2,256,512]{2,1,0:T(8,128)(2,1)S(1)}, bf16[2,256,512]{2,1,0:T(8,128)(2,1)}, u32[]{:S(2)}, u32[]{:S(2)}) collective-permute-start(bf16[2,256,512]{2,1,0:T(8,128)(2,1)S(1)} %pad_maximum_fusion.4), channel_id=1, source_target_pairs={{0,8},{8,16},{16,24},{24,32},{32,40},{40,48},{48,56},{56,64},{64,7... | collective-permute-start | bytes 1572872 | tf_op jit(solution)/shard_map/ppermute | solution.py:15
  410.7 148.4 %all-gather.17.cloned.1.call-start = ((), (), s32[]{:S(2)}) async-start(), calls=%async_computation.5 | async-start | bytes 4718592 | tf_op jit(solution)/shard_map/all_gather | solution.py:104
Sparse Core Ops, SparseCore 0:
  23.2 58.7 all-gather.6
  99.9 72.4 all-gather.8
  200.5 69.2 all-gather.10
  291.5 58.6 all-gather.12
  410.8 57.8 all-gather.14
  486.6 72.4 all-gather.16
